TPU v7x, 256 devices: a whole 4x4x8 slice. The times are simulated.
256 devices in a mesh: row: 16 (over z, core), col: 16 (over x, y).
Axes of the slice: x: 4, y: 4, z: 8, core: 2. Of those that a mesh axis runs over, the one named last changes fastest.
Arguments:
- cost_tiles: float32 [16, 16, 64, 128, 128], P('row', 'col'), may hold values from 0 to 66
- tile_rows: int32 [16, 16, 64], P('row', 'col'), may hold values from 0 to 127, as said below
- tile_cols: int32 [16, 16, 64], P('row', 'col'), may hold values from 0 to 127
- tile_count: int32 [16, 16], P('row', 'col'), may hold values from 16 to 64, as said below
- source_logmass: float32 [262144], P('row'), may hold values from -3 to 0
- target_logmass: float32 [262144], P('col'), may hold values from -103 to -100
- target_init: float32 [262144], P('col'), may hold values from -2 to 14
Outputs:
- source_potential: float32 [262144], P('row')
- target_potential: float32 [262144], P('col')
Inputs may be any that keep to these rules, and one draw needn't show every extreme that they name: Among the first tile_count slots of a device all (tile_rows, tile_cols) pairs differ; every source block of a row shard appears in such a slot of some device of that shard, and every target block of a col shard likewise. Slots at tile_count or later hold pairs to be ignored. `tile_count`: some device has all 64 slots in use in every draw.
All inputs are finite; a program needn't handle non-finite values.
Results may differ from a plain program's by a relative error of at most 0.00019.
Values sent between devices are 32-bit elements; how exact they have to be, the bound alone decides.
No kernel may reach another device: no remote copies, remote signals or barrier semaphores. Data moves between devices by JAX's collectives and lax.ppermute only.
A program may use at most 64 MiB of HBM per device.

v0:
```python
import jax
import jax.numpy as jnp
from jax import lax
from jax.sharding import PartitionSpec as P

ITERS = 2
EPS = 0.1


def copy_for_each(shard, axis):
    peers = lax.axis_size(axis)
    return lax.all_to_all(
        jnp.broadcast_to(shard[None], (peers, *shard.shape)), axis, 0, 0, tiled=True
    )


def of_everyone(shard, axis):
    everything = copy_for_each(shard, axis)
    return jnp.max(everything, axis=0)


def cut_along(shard, dim, peers):
    before, after = (shard.shape[:dim], shard.shape[dim + 1 :])
    return jnp.moveaxis(shard.reshape(*before, peers, -1, *after), dim, 0)


def sent_and_summed(shard, axis, dim):
    peers = lax.axis_size(axis)
    parts = lax.all_to_all(cut_along(shard, dim, peers), axis, 0, 0, tiled=True)
    return jnp.sum(parts, axis=0)


def in_order(parts, dim):
    shape = list(parts.shape[1:])
    shape[dim] *= parts.shape[0]
    return jnp.moveaxis(parts, 0, dim).reshape(shape)


def gathered_copies(shard, axis, dim):
    parts = copy_for_each(shard, axis)
    return in_order(parts, dim)


def block_stats(cost, pot_blocks, gather_ids, seg_ids, valid, nseg, rows_side):
    red = 2 if rows_side else 1
    part = pot_blocks[gather_ids]
    if rows_side:
        scores = (part[:, None, :] - cost) / EPS
    else:
        scores = (part[:, :, None] - cost) / EPS
    tmax = jnp.where(valid[:, None], jnp.max(scores, axis=red), -jnp.inf)
    onehot = (seg_ids[:, None] == jnp.arange(nseg)[None, :]) & valid[:, None]
    peak = jnp.max(jnp.where(onehot.T[:, :, None], tmax[None, :, :], -jnp.inf), axis=1)
    shift = jnp.where(valid[:, None], peak[seg_ids], 0.0)
    if rows_side:
        expo = jnp.exp(scores - shift[:, :, None])
    else:
        expo = jnp.exp(scores - shift[:, None, :])
    tsum = jnp.where(valid[:, None], jnp.sum(expo, axis=red), 0.0)
    mass = jnp.dot(
        onehot.astype(jnp.float32).T,
        tsum,
        precision=lax.Precision.HIGHEST,
        preferred_element_type=jnp.float32,
    )
    return (peak, mass)


def local_stats(cost, pot, gather_ids, seg_ids, count, nseg, rows_side):
    pot_blocks = pot.reshape(-1, cost.shape[-1])
    slots = cost.shape[0]
    valid = jnp.arange(slots) < count
    return block_stats(cost, pot_blocks, gather_ids, seg_ids, valid, nseg, rows_side)


def finish_source(peak, mass, logmass):
    top = of_everyone(peak, "col")
    scaled = mass * jnp.exp(peak - top)
    share = sent_and_summed(scaled.reshape(-1), "col", 0)
    width = share.shape[0]
    start = lax.axis_index("col") * width
    top_share = lax.dynamic_slice_in_dim(top.reshape(-1), start, width, 0)
    mass_share = lax.dynamic_slice_in_dim(logmass, start, width, 0)
    piece = EPS * mass_share - EPS * (top_share + jnp.log(share))
    return gathered_copies(piece, "col", 0)


def finish_target(peak, mass, logmass):
    top = of_everyone(peak, "row")
    scaled = mass * jnp.exp(peak - top)
    share = sent_and_summed(scaled.reshape(-1), "row", 0)
    width = share.shape[0]
    start = lax.axis_index("row") * width
    top_share = lax.dynamic_slice_in_dim(top.reshape(-1), start, width, 0)
    mass_share = lax.dynamic_slice_in_dim(logmass, start, width, 0)
    piece = EPS * mass_share - EPS * (top_share + jnp.log(share))
    return lax.all_gather(piece, "row", axis=0, tiled=True)


def local(
    cost_tiles, tile_rows, tile_cols, tile_count, source_logmass, target_logmass, target_init
):
    width = cost_tiles.shape[-1]
    cost = cost_tiles.reshape(cost_tiles.shape[2], width, width)
    rows = tile_rows.reshape(-1)
    cols = tile_cols.reshape(-1)
    count = tile_count.reshape(())
    src_blocks = source_logmass.shape[0] // width
    tgt_blocks = target_logmass.shape[0] // width
    target_potential = target_init
    source_potential = source_logmass
    for step in range(ITERS):
        peak, mass = local_stats(cost, target_potential, cols, rows, count, src_blocks, True)
        source_potential = finish_source(peak, mass, source_logmass)
        peak, mass = local_stats(cost, source_potential, rows, cols, count, tgt_blocks, False)
        target_potential = finish_target(peak, mass, target_logmass)
    return (source_potential, target_potential)


def solution(mesh):
    return jax.shard_map(
        local,
        mesh=mesh,
        in_specs=(
            P("row", "col", None, None, None),
            P("row", "col", None),
            P("row", "col", None),
            P("row", "col"),
            P("row"),
            P("col"),
            P("col"),
        ),
        out_specs=(P("row"), P("col")),
        check_vma=False,
    )
```

profile of v0, /device:TPU:1, one launch (start us, length us, event | category | flops | bytes accessed | tf_op | source)
XLA Modules:
  0.0 249.2 jit_solution(4396380979940419612)
XLA Ops:
  1.4 0.7 fusion.32
  2.0 0.6 gather_fusion
  2.6 3.3 %fusion.7 = f32[64,128]{1,0:T(8,128)S(1)} fusion(f32[1,1,64,128,128]{4,3,2,1,0:T(8,128)} %param.7, f32[64,128]{1,0:T(8,128)S(1)} %gather_fusion), kind=kLoop, calls=%fused_computation.27 | loop fusion | flops 3137536 | bytes 4259840 | tf_op jit(solution)/shard_map/reduce_max | solution.py:51
  6.1 1.6 select_reduce_fusion.3
  7.7 1.1 broadcast_in_dim.190
  8.8 7.6 %all-to-all-start = ((f32[16,128,128]{2,1,0:T(8,128)}), f32[16,128,128]{2,1,0:T(8,128)S(1)}, u32[]{:S(2)}, u32[]{:S(2)}) async-start(f32[16,128,128]{2,1,0:T(8,128)} %broadcast_in_dim.190), calls=%async_computation | async-start | bytes 2097152 | tf_op jit(solution)/shard_map/all_to_all | solution.py:12
  16.4 0.6 gather_fusion.1
  17.1 4.0 %exponential_reduce_fusion.3 = f32[64,128]{1,0:T(8,128)S(1)} fusion(f32[1,1,64,128,128]{4,3,2,1,0:T(8,128)} %param.7, f32[64,128]{1,0:T(8,128)S(1)} %broadcast_select_fusion.3, f32[64,128]{1,0:T(8,128)S(1)} %gather_fusion), kind=kLoop, calls=%fused_computation.22 | loop fusion | flops 4186112 | bytes 4292608 | tf_op jit(solution)/shard_map/reduce_sum | solution.py:59
  21.1 11.0 %all-to-all-done = f32[16,128,128]{2,1,0:T(8,128)S(1)} async-done(((f32[16,128,128]{2,1,0:T(8,128)}), f32[16,128,128]{2,1,0:T(8,128)S(1)}, u32[]{:S(2)}, u32[]{:S(2)}) %all-to-all-start) | async-done | bytes 1048608 | tf_op jit(solution)/shard_map/all_to_all | solution.py:12
  32.1 1.0 convolution_multiply_fusion.3
  33.1 3.9 %all-to-all-start.1 = ((f32[16,1,1024]{2,1,0:T(1,128)}), f32[16,1,1024]{2,1,0:T(1,128)S(1)}, u32[]{:S(2)}, u32[]{:S(2)}) async-start(f32[16,1,1024]{2,1,0:T(1,128)} %bitcast.10), calls=%async_computation.1 | async-start | bytes 131072 | tf_op jit(solution)/shard_map/all_to_all | solution.py:29
  37.0 6.5 %all-to-all-done.1 = f32[16,1,1024]{2,1,0:T(1,128)S(1)} async-done(((f32[16,1,1024]{2,1,0:T(1,128)}), f32[16,1,1024]{2,1,0:T(1,128)S(1)}, u32[]{:S(2)}, u32[]{:S(2)}) %all-to-all-start.1) | async-done | bytes 65568 | tf_op jit(solution)/shard_map/all_to_all | solution.py:29
  43.6 0.7 multiply_subtract_fusion.3
  44.3 9.5 %all_to_all.68 = f32[16,1,1024]{2,1,0:T(1,128)S(1)} all-to-all(f32[16,1,1024]{2,1,0:T(1,128)S(1)} %broadcast_in_dim.192), channel_id=1, replica_groups=mesh['row'=16,'col'=16] {'col'}, dimensions={0} | all-to-all | bytes 131072 | tf_op jit(solution)/shard_map/all_to_all | solution.py:12
  54.4 2.9 %fusion.6 = f32[64,128]{1,0:T(8,128)S(1)} fusion(f32[1,1,64,128,128]{4,3,2,1,0:T(8,128)} %param.7, f32[64,128]{1,0:T(8,128)S(1)} %gather_fusion.2), kind=kLoop, calls=%fused_computation.26 | loop fusion | flops 3137536 | bytes 4259840 | tf_op jit(solution)/shard_map/reduce_max | solution.py:51
  57.3 1.6 select_reduce_fusion.2
  58.9 1.1 broadcast_in_dim.194
  60.0 13.7 %all-to-all-start.3 = ((f32[16,128,128]{2,1,0:T(8,128)}), f32[16,128,128]{2,1,0:T(8,128)S(1)}, u32[]{:S(2)}, u32[]{:S(2)}) async-start(f32[16,128,128]{2,1,0:T(8,128)} %broadcast_in_dim.194), calls=%async_computation.3 | async-start | bytes 2097152 | tf_op jit(solution)/shard_map/all_to_all | solution.py:12
  74.3 2.9 %exponential_reduce_fusion.2 = f32[64,128]{1,0:T(8,128)S(1)} fusion(f32[1,1,64,128,128]{4,3,2,1,0:T(8,128)} %param.7, f32[64,128]{1,0:T(8,128)S(1)} %broadcast_select_fusion.2, f32[64,128]{1,0:T(8,128)S(1)} %gather_fusion.2), kind=kLoop, calls=%fused_computation.20 | loop fusion | flops 4186112 | bytes 4292608 | tf_op jit(solution)/shard_map/reduce_sum | solution.py:59
  77.3 24.4 %all-to-all-done.3 = f32[16,128,128]{2,1,0:T(8,128)S(1)} async-done(((f32[16,128,128]{2,1,0:T(8,128)}), f32[16,128,128]{2,1,0:T(8,128)S(1)}, u32[]{:S(2)}, u32[]{:S(2)}) %all-to-all-start.3) | async-done | bytes 1048608 | tf_op jit(solution)/shard_map/all_to_all | solution.py:12
  101.7 1.0 convolution_multiply_fusion.2
  102.7 3.4 %all-to-all-start.4 = ((f32[16,1,1024]{2,1,0:T(1,128)}), f32[16,1,1024]{2,1,0:T(1,128)S(1)}, u32[]{:S(2)}, u32[]{:S(2)}) async-start(f32[16,1,1024]{2,1,0:T(1,128)} %bitcast.13), calls=%async_computation.4 | async-start | bytes 131072 | tf_op jit(solution)/shard_map/all_to_all | solution.py:29
  106.1 7.8 %all-to-all-done.4 = f32[16,1,1024]{2,1,0:T(1,128)S(1)} async-done(((f32[16,1,1024]{2,1,0:T(1,128)}), f32[16,1,1024]{2,1,0:T(1,128)S(1)}, u32[]{:S(2)}, u32[]{:S(2)}) %all-to-all-start.4) | async-done | bytes 65568 | tf_op jit(solution)/shard_map/all_to_all | solution.py:29
  113.9 0.7 multiply_subtract_fusion.2
  114.6 14.9 %all_gather.6 = f32[16384]{0:T(1024)S(1)} all-gather(f32[1024]{0:T(1024)S(1)} %multiply_subtract_fusion.2), channel_id=1, replica_groups=mesh['row'=16,'col'=16] {'row'}, dimensions={0}, use_global_device_ids=true | all-gather | bytes 69632 | tf_op jit(solution)/shard_map/all_gather | solution.py:97
  130.1 3.3 %fusion.5 = f32[64,128]{1,0:T(8,128)S(1)} fusion(f32[1,1,64,128,128]{4,3,2,1,0:T(8,128)} %param.7, f32[64,128]{1,0:T(8,128)S(1)} %gather_fusion.4), kind=kLoop, calls=%fused_computation.25 | loop fusion | flops 3137536 | bytes 4259840 | tf_op jit(solution)/shard_map/reduce_max | solution.py:51
  133.5 1.6 select_reduce_fusion.1
  135.1 1.1 broadcast_in_dim.196
  136.2 3.7 %all-to-all-start.5 = ((f32[16,128,128]{2,1,0:T(8,128)}), f32[16,128,128]{2,1,0:T(8,128)S(1)}, u32[]{:S(2)}, u32[]{:S(2)}) async-start(f32[16,128,128]{2,1,0:T(8,128)} %broadcast_in_dim.196), calls=%async_computation.5 | async-start | bytes 2097152 | tf_op jit(solution)/shard_map/all_to_all | solution.py:12
  139.9 0.6 gather_fusion.5
  140.6 4.0 %exponential_reduce_fusion.1 = f32[64,128]{1,0:T(8,128)S(1)} fusion(f32[1,1,64,128,128]{4,3,2,1,0:T(8,128)} %param.7, f32[64,128]{1,0:T(8,128)S(1)} %broadcast_select_fusion.1, f32[64,128]{1,0:T(8,128)S(1)} %gather_fusion.4), kind=kLoop, calls=%fused_computation.18 | loop fusion | flops 4186112 | bytes 4292608 | tf_op jit(solution)/shard_map/reduce_sum | solution.py:59
  144.5 12.5 %all-to-all-done.5 = f32[16,128,128]{2,1,0:T(8,128)S(1)} async-done(((f32[16,128,128]{2,1,0:T(8,128)}), f32[16,128,128]{2,1,0:T(8,128)S(1)}, u32[]{:S(2)}, u32[]{:S(2)}) %all-to-all-start.5) | async-done | bytes 1048608 | tf_op jit(solution)/shard_map/all_to_all | solution.py:12
  157.4 9.8 %all_to_all.69 = f32[16,1,1024]{2,1,0:T(1,128)S(1)} all-to-all(f32[16,1,1024]{2,1,0:T(1,128)S(1)} %bitcast.63), channel_id=1, replica_groups=mesh['row'=16,'col'=16] {'col'}, dimensions={0} | all-to-all | bytes 131072 | tf_op jit(solution)/shard_map/all_to_all | solution.py:29
  167.3 0.7 multiply_subtract_fusion.1
  168.0 9.8 %all_to_all.70 = f32[16,1,1024]{2,1,0:T(1,128)S(1)} all-to-all(f32[16,1,1024]{2,1,0:T(1,128)S(1)} %broadcast_in_dim.197), channel_id=1, replica_groups=mesh['row'=16,'col'=16] {'col'}, dimensions={0} | all-to-all | bytes 131072 | tf_op jit(solution)/shard_map/all_to_all | solution.py:12
  178.4 2.8 %fusion.4 = f32[64,128]{1,0:T(8,128)S(1)} fusion(f32[1,1,64,128,128]{4,3,2,1,0:T(8,128)} %param.7, f32[64,128]{1,0:T(8,128)S(1)} %gather_fusion.6), kind=kLoop, calls=%fused_computation.24 | loop fusion | flops 3137536 | bytes 4259840 | tf_op jit(solution)/shard_map/reduce_max | solution.py:51
  181.3 1.6 select_reduce_fusion
  182.9 1.1 broadcast_in_dim.199
  184.0 8.1 %all-to-all-start.8 = ((f32[16,128,128]{2,1,0:T(8,128)}), f32[16,128,128]{2,1,0:T(8,128)S(1)}, u32[]{:S(2)}, u32[]{:S(2)}) async-start(f32[16,128,128]{2,1,0:T(8,128)} %broadcast_in_dim.199), calls=%async_computation.8 | async-start | bytes 2097152 | tf_op jit(solution)/shard_map/all_to_all | solution.py:12
  192.8 2.9 %exponential_reduce_fusion = f32[64,128]{1,0:T(8,128)S(1)} fusion(f32[1,1,64,128,128]{4,3,2,1,0:T(8,128)} %param.7, f32[64,128]{1,0:T(8,128)S(1)} %broadcast_select_fusion, f32[64,128]{1,0:T(8,128)S(1)} %gather_fusion.6), kind=kLoop, calls=%fused_computation.16 | loop fusion | flops 4186112 | bytes 4292608 | tf_op jit(solution)/shard_map/reduce_sum | solution.py:59
  195.7 24.4 %all-to-all-done.8 = f32[16,128,128]{2,1,0:T(8,128)S(1)} async-done(((f32[16,128,128]{2,1,0:T(8,128)}), f32[16,128,128]{2,1,0:T(8,128)S(1)}, u32[]{:S(2)}, u32[]{:S(2)}) %all-to-all-start.8) | async-done | bytes 1048608 | tf_op jit(solution)/shard_map/all_to_all | solution.py:12
  220.1 1.0 convolution_multiply_fusion
  221.1 3.4 %all-to-all-start.9 = ((f32[16,1,1024]{2,1,0:T(1,128)}), f32[16,1,1024]{2,1,0:T(1,128)S(1)}, u32[]{:S(2)}, u32[]{:S(2)}) async-start(f32[16,1,1024]{2,1,0:T(1,128)} %bitcast.20), calls=%async_computation.9 | async-start | bytes 131072 | tf_op jit(solution)/shard_map/all_to_all | solution.py:29
  224.5 7.8 %all-to-all-done.9 = f32[16,1,1024]{2,1,0:T(1,128)S(1)} async-done(((f32[16,1,1024]{2,1,0:T(1,128)}), f32[16,1,1024]{2,1,0:T(1,128)S(1)}, u32[]{:S(2)}, u32[]{:S(2)}) %all-to-all-start.9) | async-done | bytes 65568 | tf_op jit(solution)/shard_map/all_to_all | solution.py:29
  232.4 0.7 multiply_subtract_fusion
  233.1 14.9 %all_gather.7 = f32[16384]{0:T(1024)S(1)} all-gather(f32[1024]{0:T(1024)S(1)} %multiply_subtract_fusion), channel_id=1, replica_groups=mesh['row'=16,'col'=16] {'row'}, dimensions={0}, use_global_device_ids=true | all-gather | bytes 69632 | tf_op jit(solution)/shard_map/all_gather | solution.py:97
  247.9 0.6 copy.20
  248.6 0.6 copy.21
  (35 shorter events, 4.5 us)
Async XLA Ops:
  0.6 1.4 copy-start
  0.6 5.4 %copy-start.2 = (s32[1,1,64]{2,1,0:T(1,128)S(1)}, s32[1,1,64]{2,1,0:T(1,128)}, u32[]{:S(2)}) copy-start(s32[1,1,64]{2,1,0:T(1,128)} %param.9) | copy-start | bytes 772
  0.7 5.4 %copy-start.1 = (s32[1,1,64]{2,1,0:T(1,128)S(1)}, s32[1,1,64]{2,1,0:T(1,128)}, u32[]{:S(2)}) copy-start(s32[1,1,64]{2,1,0:T(1,128)} %param.8) | copy-start | bytes 772
  8.8 23.2 %all-to-all-start = ((f32[16,128,128]{2,1,0:T(8,128)}), f32[16,128,128]{2,1,0:T(8,128)S(1)}, u32[]{:S(2)}, u32[]{:S(2)}) async-start(f32[16,128,128]{2,1,0:T(8,128)} %broadcast_in_dim.190), calls=%async_computation | async-start | bytes 2097152 | tf_op jit(solution)/shard_map/all_to_all | solution.py:12
  33.1 10.4 %all-to-all-start.1 = ((f32[16,1,1024]{2,1,0:T(1,128)}), f32[16,1,1024]{2,1,0:T(1,128)S(1)}, u32[]{:S(2)}, u32[]{:S(2)}) async-start(f32[16,1,1024]{2,1,0:T(1,128)} %bitcast.10), calls=%async_computation.1 | async-start | bytes 131072 | tf_op jit(solution)/shard_map/all_to_all | solution.py:29
  60.0 41.7 %all-to-all-start.3 = ((f32[16,128,128]{2,1,0:T(8,128)}), f32[16,128,128]{2,1,0:T(8,128)S(1)}, u32[]{:S(2)}, u32[]{:S(2)}) async-start(f32[16,128,128]{2,1,0:T(8,128)} %broadcast_in_dim.194), calls=%async_computation.3 | async-start | bytes 2097152 | tf_op jit(solution)/shard_map/all_to_all | solution.py:12
  102.7 11.2 %all-to-all-start.4 = ((f32[16,1,1024]{2,1,0:T(1,128)}), f32[16,1,1024]{2,1,0:T(1,128)S(1)}, u32[]{:S(2)}, u32[]{:S(2)}) async-start(f32[16,1,1024]{2,1,0:T(1,128)} %bitcast.13), calls=%async_computation.4 | async-start | bytes 131072 | tf_op jit(solution)/shard_map/all_to_all | solution.py:29
  136.2 20.8 %all-to-all-start.5 = ((f32[16,128,128]{2,1,0:T(8,128)}), f32[16,128,128]{2,1,0:T(8,128)S(1)}, u32[]{:S(2)}, u32[]{:S(2)}) async-start(f32[16,128,128]{2,1,0:T(8,128)} %broadcast_in_dim.196), calls=%async_computation.5 | async-start | bytes 2097152 | tf_op jit(solution)/shard_map/all_to_all | solution.py:12
  184.0 36.1 %all-to-all-start.8 = ((f32[16,128,128]{2,1,0:T(8,128)}), f32[16,128,128]{2,1,0:T(8,128)S(1)}, u32[]{:S(2)}, u32[]{:S(2)}) async-start(f32[16,128,128]{2,1,0:T(8,128)} %broadcast_in_dim.199), calls=%async_computation.8 | async-start | bytes 2097152 | tf_op jit(solution)/shard_map/all_to_all | solution.py:12
  221.1 11.2 %all-to-all-start.9 = ((f32[16,1,1024]{2,1,0:T(1,128)}), f32[16,1,1024]{2,1,0:T(1,128)S(1)}, u32[]{:S(2)}, u32[]{:S(2)}) async-start(f32[16,1,1024]{2,1,0:T(1,128)} %bitcast.20), calls=%async_computation.9 | async-start | bytes 131072 | tf_op jit(solution)/shard_map/all_to_all | solution.py:29
where the time goes:
time: 250 us; the launch traced here: 249 us
  waiting for transfers between devices  94.4 us (38%)
  blocking collectives  58.7 us (23%)
  starting transfers between devices  43.8 us (18%)
  other arithmetic  37.1 us (15%)
  local copies, waits for them, and re-layouts  10.5 us (4%)
  matrix products  3.19 us (1%)
    all_to_all x4, waiting for transfers between devices, copy_for_each(): lax.all_to_all(jnp.broadcast_to(shard[None], (peers, *shard.shape)), axis...  72.3 us
    all_to_all x4, starting transfers between devices, copy_for_each(): lax.all_to_all(jnp.broadcast_to(shard[None], (peers, *shard.shape)), axis...  33 us
    all_gather x2, blocking collectives, finish_target(): return lax.all_gather(piece, 'row', axis=0, tiled=True)  29.7 us
    all_to_all x3, waiting for transfers between devices, sent_and_summed(): parts = lax.all_to_all(cut_along(shard, dim, peers), axis, 0, 0, tiled=True)  22.1 us
    all_to_all x2, blocking collectives, copy_for_each(): lax.all_to_all(jnp.broadcast_to(shard[None], (peers, *shard.shape)), axis...  19.2 us
    reduce_sum x4, other arithmetic, block_stats(): tsum = jnp.where(valid[:, None], jnp.sum(expo, axis=red), 0.0)  13.8 us
    reduce_max x4, other arithmetic, block_stats(): tmax = jnp.where(valid[:, None], jnp.max(scores, axis=red), -jnp.inf)  12.4 us
    all_to_all x3, starting transfers between devices, sent_and_summed(): parts = lax.all_to_all(cut_along(shard, dim, peers), axis, 0, 0, tiled=True)  10.8 us
  transfers between devices with their start and end apart: 7, of which 7 were waited for; matrix products, arithmetic and copies ran while one was open for 7% of the time, Pallas kernels for 0%

commit v1 on v0

--- a/solution.py
+++ b/solution.py
@@ -1,3 +1,4 @@
+import functools
 import jax
 import jax.numpy as jnp
 from jax import lax
@@ -5,6 +6,15 @@
 
 ITERS = 2
 EPS = 0.1
+
+
+def manage_panel(local_x, dim_at):
+    return jnp.concatenate(
+        lax.all_to_all(jnp.stack([local_x] * lax.psum(1, "row"), 0), "row", 0, 0), dim_at
+    )
+
+
+carry_stops_all = functools.partial(manage_panel, dim_at=0)
 
 
 def copy_for_each(shard, axis):
@@ -94,7 +104,7 @@
     top_share = lax.dynamic_slice_in_dim(top.reshape(-1), start, width, 0)
     mass_share = lax.dynamic_slice_in_dim(logmass, start, width, 0)
     piece = EPS * mass_share - EPS * (top_share + jnp.log(share))
-    return lax.all_gather(piece, "row", axis=0, tiled=True)
+    return carry_stops_all(piece)
 
 
 def local(

time: 250 us -> 241 us (0.964)
  blocking collectives: 58.7 us -> 50.3 us
    all_gather x2 -> x0, blocking collectives: 29.7 us -> none  [finish_target(): return lax.all_gather(piece, 'row', axis=0, tiled=True)]
    all_to_all x1 -> x2, blocking collectives: 9.76 us -> 20.7 us  [sent_and_summed(): parts = lax.all_to_all(cut_along(shard, dim, peers), axis, 0, 0, tiled=True)]
    all_to_all x0 -> x1, blocking collectives: none -> 10.3 us  [manage_panel(): lax.all_to_all(jnp.stack([local_x] * lax.psum(1, 'row'), 0), 'row', 0, 0)]
    all_to_all x0 -> x1, waiting for transfers between devices: none -> 7.82 us  [manage_panel(): lax.all_to_all(jnp.stack([local_x] * lax.psum(1, 'row'), 0), 'row', 0, 0)]
    all_to_all x3 -> x2, waiting for transfers between devices: 22.1 us -> 14.3 us  [sent_and_summed(): parts = lax.all_to_all(cut_along(shard, dim, peers), axis, 0, 0, tiled=True)]
    all_to_all x3 -> x2, starting transfers between devices: 10.8 us -> 7.33 us  [sent_and_summed(): parts = lax.all_to_all(cut_along(shard, dim, peers), axis, 0, 0, tiled=True)]
    all_to_all x0 -> x1, starting transfers between devices: none -> 3.41 us  [manage_panel(): lax.all_to_all(jnp.stack([local_x] * lax.psum(1, 'row'), 0), 'row', 0, 0)]
where the time goes in v1:
time: 241 us; the launch traced here: 240 us
  waiting for transfers between devices  94.5 us (39%)
  blocking collectives  50.3 us (21%)
  starting transfers between devices  43 us (18%)
  other arithmetic  37.1 us (15%)
  local copies, waits for them, and re-layouts  11.2 us (5%)
  matrix products  2.56 us (1%)
    all_to_all x4, waiting for transfers between devices, copy_for_each(): lax.all_to_all(jnp.broadcast_to(shard[None], (peers, *shard.shape)), axis...  72.4 us
    all_to_all x4, starting transfers between devices, copy_for_each(): lax.all_to_all(jnp.broadcast_to(shard[None], (peers, *shard.shape)), axis...  32.2 us
    all_to_all x2, blocking collectives, sent_and_summed(): parts = lax.all_to_all(cut_along(shard, dim, peers), axis, 0, 0, tiled=True)  20.7 us
    all_to_all x2, blocking collectives, copy_for_each(): lax.all_to_all(jnp.broadcast_to(shard[None], (peers, *shard.shape)), axis...  19.2 us
    all_to_all x2, waiting for transfers between devices, sent_and_summed(): parts = lax.all_to_all(cut_along(shard, dim, peers), axis, 0, 0, tiled=True)  14.3 us
    reduce_sum x4, other arithmetic, block_stats(): tsum = jnp.where(valid[:, None], jnp.sum(expo, axis=red), 0.0)  13.8 us
    reduce_max x4, other arithmetic, block_stats(): tmax = jnp.where(valid[:, None], jnp.max(scores, axis=red), -jnp.inf)  12.4 us
    all_to_all x1, blocking collectives, manage_panel(): lax.all_to_all(jnp.stack([local_x] * lax.psum(1, 'row'), 0), 'row', 0, 0)  10.3 us
  transfers between devices with their start and end apart: 7, of which 7 were waited for; matrix products, arithmetic and copies ran while one was open for 7% of the time, Pallas kernels for 0%

profile of v1, /device:TPU:1, one launch (start us, length us, event | category | flops | bytes accessed | tf_op | source)
XLA Modules:
  0.0 240.2 jit_solution(5336740138680823560)
XLA Ops:
  1.4 0.7 fusion.32
  2.0 0.6 gather_fusion
  2.6 3.3 %fusion.7 = f32[64,128]{1,0:T(8,128)S(1)} fusion(f32[1,1,64,128,128]{4,3,2,1,0:T(8,128)} %param.7, f32[64,128]{1,0:T(8,128)S(1)} %gather_fusion), kind=kLoop, calls=%fused_computation.27 | loop fusion | flops 3137536 | bytes 4259840 | tf_op jit(solution)/shard_map/reduce_max | solution.py:61
  6.1 1.6 select_reduce_fusion.3
  7.7 1.1 broadcast_in_dim.190
  8.8 7.6 %all-to-all-start = ((f32[16,128,128]{2,1,0:T(8,128)}), f32[16,128,128]{2,1,0:T(8,128)S(1)}, u32[]{:S(2)}, u32[]{:S(2)}) async-start(f32[16,128,128]{2,1,0:T(8,128)} %broadcast_in_dim.190), calls=%async_computation | async-start | bytes 2097152 | tf_op jit(solution)/shard_map/all_to_all | solution.py:22
  16.4 0.6 gather_fusion.1
  17.1 4.0 %exponential_reduce_fusion.3 = f32[64,128]{1,0:T(8,128)S(1)} fusion(f32[1,1,64,128,128]{4,3,2,1,0:T(8,128)} %param.7, f32[64,128]{1,0:T(8,128)S(1)} %broadcast_select_fusion.3, f32[64,128]{1,0:T(8,128)S(1)} %gather_fusion), kind=kLoop, calls=%fused_computation.22 | loop fusion | flops 4186112 | bytes 4292608 | tf_op jit(solution)/shard_map/reduce_sum | solution.py:69
  21.1 11.0 %all-to-all-done = f32[16,128,128]{2,1,0:T(8,128)S(1)} async-done(((f32[16,128,128]{2,1,0:T(8,128)}), f32[16,128,128]{2,1,0:T(8,128)S(1)}, u32[]{:S(2)}, u32[]{:S(2)}) %all-to-all-start) | async-done | bytes 1048608 | tf_op jit(solution)/shard_map/all_to_all | solution.py:22
  32.1 1.0 convolution_multiply_fusion.3
  33.1 3.9 %all-to-all-start.1 = ((f32[16,1,1024]{2,1,0:T(1,128)}), f32[16,1,1024]{2,1,0:T(1,128)S(1)}, u32[]{:S(2)}, u32[]{:S(2)}) async-start(f32[16,1,1024]{2,1,0:T(1,128)} %bitcast.10), calls=%async_computation.1 | async-start | bytes 131072 | tf_op jit(solution)/shard_map/all_to_all | solution.py:39
  37.0 6.5 %all-to-all-done.1 = f32[16,1,1024]{2,1,0:T(1,128)S(1)} async-done(((f32[16,1,1024]{2,1,0:T(1,128)}), f32[16,1,1024]{2,1,0:T(1,128)S(1)}, u32[]{:S(2)}, u32[]{:S(2)}) %all-to-all-start.1) | async-done | bytes 65568 | tf_op jit(solution)/shard_map/all_to_all | solution.py:39
  43.6 0.7 multiply_subtract_fusion.3
  44.3 9.5 %all_to_all.80 = f32[16,1,1024]{2,1,0:T(1,128)S(1)} all-to-all(f32[16,1,1024]{2,1,0:T(1,128)S(1)} %broadcast_in_dim.192), channel_id=1, replica_groups=mesh['row'=16,'col'=16] {'col'}, dimensions={0} | all-to-all | bytes 131072 | tf_op jit(solution)/shard_map/all_to_all | solution.py:22
  54.4 2.9 %fusion.6 = f32[64,128]{1,0:T(8,128)S(1)} fusion(f32[1,1,64,128,128]{4,3,2,1,0:T(8,128)} %param.7, f32[64,128]{1,0:T(8,128)S(1)} %gather_fusion.2), kind=kLoop, calls=%fused_computation.26 | loop fusion | flops 3137536 | bytes 4259840 | tf_op jit(solution)/shard_map/reduce_max | solution.py:61
  57.3 1.6 select_reduce_fusion.2
  58.9 1.1 broadcast_in_dim.194
  60.0 13.7 %all-to-all-start.3 = ((f32[16,128,128]{2,1,0:T(8,128)}), f32[16,128,128]{2,1,0:T(8,128)S(1)}, u32[]{:S(2)}, u32[]{:S(2)}) async-start(f32[16,128,128]{2,1,0:T(8,128)} %broadcast_in_dim.194), calls=%async_computation.3 | async-start | bytes 2097152 | tf_op jit(solution)/shard_map/all_to_all | solution.py:22
  74.3 2.9 %exponential_reduce_fusion.2 = f32[64,128]{1,0:T(8,128)S(1)} fusion(f32[1,1,64,128,128]{4,3,2,1,0:T(8,128)} %param.7, f32[64,128]{1,0:T(8,128)S(1)} %broadcast_select_fusion.2, f32[64,128]{1,0:T(8,128)S(1)} %gather_fusion.2), kind=kLoop, calls=%fused_computation.20 | loop fusion | flops 4186112 | bytes 4292608 | tf_op jit(solution)/shard_map/reduce_sum | solution.py:69
  77.3 24.4 %all-to-all-done.3 = f32[16,128,128]{2,1,0:T(8,128)S(1)} async-done(((f32[16,128,128]{2,1,0:T(8,128)}), f32[16,128,128]{2,1,0:T(8,128)S(1)}, u32[]{:S(2)}, u32[]{:S(2)}) %all-to-all-start.3) | async-done | bytes 1048608 | tf_op jit(solution)/shard_map/all_to_all | solution.py:22
  101.7 1.0 convolution_multiply_fusion.2
  102.7 3.4 %all-to-all-start.4 = ((f32[16,1,1024]{2,1,0:T(1,128)}), f32[16,1,1024]{2,1,0:T(1,128)S(1)}, u32[]{:S(2)}, u32[]{:S(2)}) async-start(f32[16,1,1024]{2,1,0:T(1,128)} %bitcast.13), calls=%async_computation.4 | async-start | bytes 131072 | tf_op jit(solution)/shard_map/all_to_all | solution.py:39
  106.1 7.8 %all-to-all-done.4 = f32[16,1,1024]{2,1,0:T(1,128)S(1)} async-done(((f32[16,1,1024]{2,1,0:T(1,128)}), f32[16,1,1024]{2,1,0:T(1,128)S(1)}, u32[]{:S(2)}, u32[]{:S(2)}) %all-to-all-start.4) | async-done | bytes 65568 | tf_op jit(solution)/shard_map/all_to_all | solution.py:39
  113.9 0.7 multiply_subtract_fusion.2
  114.7 10.3 %all_to_all.81 = f32[16,1,1024]{2,1,0:T(1,128)S(1)} all-to-all(f32[16,1,1024]{2,1,0:T(1,128)S(1)} %stack.4), channel_id=1, replica_groups=mesh['row'=16,'col'=16] {'row'}, dimensions={0} | all-to-all | bytes 131072 | tf_op jit(solution)/shard_map/all_to_all | solution.py:13
  125.6 3.3 %fusion.5 = f32[64,128]{1,0:T(8,128)S(1)} fusion(f32[1,1,64,128,128]{4,3,2,1,0:T(8,128)} %param.7, f32[64,128]{1,0:T(8,128)S(1)} %gather_fusion.4), kind=kLoop, calls=%fused_computation.25 | loop fusion | flops 3137536 | bytes 4259840 | tf_op jit(solution)/shard_map/reduce_max | solution.py:61
  129.0 1.6 select_reduce_fusion.1
  130.7 1.1 broadcast_in_dim.196
  131.7 3.7 %all-to-all-start.6 = ((f32[16,128,128]{2,1,0:T(8,128)}), f32[16,128,128]{2,1,0:T(8,128)S(1)}, u32[]{:S(2)}, u32[]{:S(2)}) async-start(f32[16,128,128]{2,1,0:T(8,128)} %broadcast_in_dim.196), calls=%async_computation.6 | async-start | bytes 2097152 | tf_op jit(solution)/shard_map/all_to_all | solution.py:22
  135.4 0.6 gather_fusion.5
  136.1 4.0 %exponential_reduce_fusion.1 = f32[64,128]{1,0:T(8,128)S(1)} fusion(f32[1,1,64,128,128]{4,3,2,1,0:T(8,128)} %param.7, f32[64,128]{1,0:T(8,128)S(1)} %broadcast_select_fusion.1, f32[64,128]{1,0:T(8,128)S(1)} %gather_fusion.4), kind=kLoop, calls=%fused_computation.18 | loop fusion | flops 4186112 | bytes 4292608 | tf_op jit(solution)/shard_map/reduce_sum | solution.py:69
  140.1 12.5 %all-to-all-done.6 = f32[16,128,128]{2,1,0:T(8,128)S(1)} async-done(((f32[16,128,128]{2,1,0:T(8,128)}), f32[16,128,128]{2,1,0:T(8,128)S(1)}, u32[]{:S(2)}, u32[]{:S(2)}) %all-to-all-start.6) | async-done | bytes 1048608 | tf_op jit(solution)/shard_map/all_to_all | solution.py:22
  153.0 9.7 %all_to_all.82 = f32[16,1,1024]{2,1,0:T(1,128)S(1)} all-to-all(f32[16,1,1024]{2,1,0:T(1,128)S(1)} %bitcast.65), channel_id=1, replica_groups=mesh['row'=16,'col'=16] {'col'}, dimensions={0} | all-to-all | bytes 131072 | tf_op jit(solution)/shard_map/all_to_all | solution.py:39
  162.8 0.7 multiply_subtract_fusion.1
  163.5 9.8 %all_to_all.83 = f32[16,1,1024]{2,1,0:T(1,128)S(1)} all-to-all(f32[16,1,1024]{2,1,0:T(1,128)S(1)} %broadcast_in_dim.197), channel_id=1, replica_groups=mesh['row'=16,'col'=16] {'col'}, dimensions={0} | all-to-all | bytes 131072 | tf_op jit(solution)/shard_map/all_to_all | solution.py:22
  173.9 2.8 %fusion.4 = f32[64,128]{1,0:T(8,128)S(1)} fusion(f32[1,1,64,128,128]{4,3,2,1,0:T(8,128)} %param.7, f32[64,128]{1,0:T(8,128)S(1)} %gather_fusion.6), kind=kLoop, calls=%fused_computation.24 | loop fusion | flops 3137536 | bytes 4259840 | tf_op jit(solution)/shard_map/reduce_max | solution.py:61
  176.8 1.6 select_reduce_fusion
  178.4 1.1 broadcast_in_dim.199
  179.5 7.3 %all-to-all-start.9 = ((f32[16,128,128]{2,1,0:T(8,128)}), f32[16,128,128]{2,1,0:T(8,128)S(1)}, u32[]{:S(2)}, u32[]{:S(2)}) async-start(f32[16,128,128]{2,1,0:T(8,128)} %broadcast_in_dim.199), calls=%async_computation.9 | async-start | bytes 2097152 | tf_op jit(solution)/shard_map/all_to_all | solution.py:22
  187.5 2.9 %exponential_reduce_fusion = f32[64,128]{1,0:T(8,128)S(1)} fusion(f32[1,1,64,128,128]{4,3,2,1,0:T(8,128)} %param.7, f32[64,128]{1,0:T(8,128)S(1)} %broadcast_select_fusion, f32[64,128]{1,0:T(8,128)S(1)} %gather_fusion.6), kind=kLoop, calls=%fused_computation.16 | loop fusion | flops 4186112 | bytes 4292608 | tf_op jit(solution)/shard_map/reduce_sum | solution.py:69
  190.4 24.5 %all-to-all-done.9 = f32[16,128,128]{2,1,0:T(8,128)S(1)} async-done(((f32[16,128,128]{2,1,0:T(8,128)}), f32[16,128,128]{2,1,0:T(8,128)S(1)}, u32[]{:S(2)}, u32[]{:S(2)}) %all-to-all-start.9) | async-done | bytes 1048608 | tf_op jit(solution)/shard_map/all_to_all | solution.py:22
  215.3 11.0 %all_to_all.84 = f32[16,1,1024]{2,1,0:T(1,128)S(1)} all-to-all(f32[16,1,1024]{2,1,0:T(1,128)S(1)} %bitcast.64), channel_id=1, replica_groups=mesh['row'=16,'col'=16] {'row'}, dimensions={0} | all-to-all | bytes 131072 | tf_op jit(solution)/shard_map/all_to_all | solution.py:39
  226.3 0.7 multiply_subtract_fusion
  227.0 0.7 stack.5
  227.7 3.4 %all-to-all-start.11 = ((f32[16,1,1024]{2,1,0:T(1,128)}), f32[16,1,1024]{2,1,0:T(1,128)S(1)}, u32[]{:S(2)}, u32[]{:S(2)}) async-start(f32[16,1,1024]{2,1,0:T(1,128)} %stack.5), calls=%async_computation.11 | async-start | bytes 131072 | tf_op jit(solution)/shard_map/all_to_all | solution.py:13
  231.1 7.8 %all-to-all-done.11 = f32[16,1,1024]{2,1,0:T(1,128)S(1)} async-done(((f32[16,1,1024]{2,1,0:T(1,128)}), f32[16,1,1024]{2,1,0:T(1,128)S(1)}, u32[]{:S(2)}, u32[]{:S(2)}) %all-to-all-start.11) | async-done | bytes 65568 | tf_op jit(solution)/shard_map/all_to_all | solution.py:13
  238.9 0.6 copy.20
  239.6 0.6 copy.21
  (37 shorter events, 4.8 us)
Async XLA Ops:
  0.6 1.4 copy-start
  0.6 5.4 %copy-start.2 = (s32[1,1,64]{2,1,0:T(1,128)S(1)}, s32[1,1,64]{2,1,0:T(1,128)}, u32[]{:S(2)}) copy-start(s32[1,1,64]{2,1,0:T(1,128)} %param.9) | copy-start | bytes 772
  0.7 5.4 %copy-start.1 = (s32[1,1,64]{2,1,0:T(1,128)S(1)}, s32[1,1,64]{2,1,0:T(1,128)}, u32[]{:S(2)}) copy-start(s32[1,1,64]{2,1,0:T(1,128)} %param.8) | copy-start | bytes 772
  8.8 23.2 %all-to-all-start = ((f32[16,128,128]{2,1,0:T(8,128)}), f32[16,128,128]{2,1,0:T(8,128)S(1)}, u32[]{:S(2)}, u32[]{:S(2)}) async-start(f32[16,128,128]{2,1,0:T(8,128)} %broadcast_in_dim.190), calls=%async_computation | async-start | bytes 2097152 | tf_op jit(solution)/shard_map/all_to_all | solution.py:22
  33.1 10.4 %all-to-all-start.1 = ((f32[16,1,1024]{2,1,0:T(1,128)}), f32[16,1,1024]{2,1,0:T(1,128)S(1)}, u32[]{:S(2)}, u32[]{:S(2)}) async-start(f32[16,1,1024]{2,1,0:T(1,128)} %bitcast.10), calls=%async_computation.1 | async-start | bytes 131072 | tf_op jit(solution)/shard_map/all_to_all | solution.py:39
  60.0 41.7 %all-to-all-start.3 = ((f32[16,128,128]{2,1,0:T(8,128)}), f32[16,128,128]{2,1,0:T(8,128)S(1)}, u32[]{:S(2)}, u32[]{:S(2)}) async-start(f32[16,128,128]{2,1,0:T(8,128)} %broadcast_in_dim.194), calls=%async_computation.3 | async-start | bytes 2097152 | tf_op jit(solution)/shard_map/all_to_all | solution.py:22
  102.7 11.2 %all-to-all-start.4 = ((f32[16,1,1024]{2,1,0:T(1,128)}), f32[16,1,1024]{2,1,0:T(1,128)S(1)}, u32[]{:S(2)}, u32[]{:S(2)}) async-start(f32[16,1,1024]{2,1,0:T(1,128)} %bitcast.13), calls=%async_computation.4 | async-start | bytes 131072 | tf_op jit(solution)/shard_map/all_to_all | solution.py:39
  131.7 20.9 %all-to-all-start.6 = ((f32[16,128,128]{2,1,0:T(8,128)}), f32[16,128,128]{2,1,0:T(8,128)S(1)}, u32[]{:S(2)}, u32[]{:S(2)}) async-start(f32[16,128,128]{2,1,0:T(8,128)} %broadcast_in_dim.196), calls=%async_computation.6 | async-start | bytes 2097152 | tf_op jit(solution)/shard_map/all_to_all | solution.py:22
  179.5 35.4 %all-to-all-start.9 = ((f32[16,128,128]{2,1,0:T(8,128)}), f32[16,128,128]{2,1,0:T(8,128)S(1)}, u32[]{:S(2)}, u32[]{:S(2)}) async-start(f32[16,128,128]{2,1,0:T(8,128)} %broadcast_in_dim.199), calls=%async_computation.9 | async-start | bytes 2097152 | tf_op jit(solution)/shard_map/all_to_all | solution.py:22
  227.7 11.2 %all-to-all-start.11 = ((f32[16,1,1024]{2,1,0:T(1,128)}), f32[16,1,1024]{2,1,0:T(1,128)S(1)}, u32[]{:S(2)}, u32[]{:S(2)}) async-start(f32[16,1,1024]{2,1,0:T(1,128)} %stack.5), calls=%async_computation.11 | async-start | bytes 131072 | tf_op jit(solution)/shard_map/all_to_all | solution.py:13
